TPU v7x, 128 devices: a whole 4x4x4 slice. The times are simulated.
128 devices in a mesh: dp: 8 (over y_lo, z), ctx: 16 (over y_hi, x, core).
Axes of the slice: x: 4, y: 4 (y_hi: 2, y_lo: 2; y = y_hi * 2 + y_lo), z: 4, core: 2. Of those that a mesh axis runs over, the one named last changes fastest.
Arguments:
- queries: bfloat16 [65536, 2048], P(('dp', 'ctx')), parts along dimension 0, may hold values from -72 to 72
- key_rows: bfloat16 [65536, 1024], P(('dp', 'ctx')), parts along dimension 0, may hold values from -6 to 6
- value_rows: bfloat16 [65536, 1024], P(('dp', 'ctx')), parts along dimension 0, may hold values from -6 to 6
- parents: int32 [512], P('dp'), parts along dimension 0, may hold values from 0 to 62, as said below
- kept_tiles: int32 [512], P('dp'), parts along dimension 0, may hold values from 0 to 1, as said below
Outputs:
- attended: bfloat16 [65536, 2048], P(('dp', 'ctx')), parts along dimension 0
There are 8 independent parts, one for each index of `dp`. A program takes and returns all parts, laid end to end along the dimension named above; each array names one. Nothing has to cross between parts.
Inputs may be any that keep to these rules, and one draw needn't show every extreme that they name: parents[b] is one to three less than b for b > 0, and parents[0] = 0. `kept_tiles`: 1 keeps a tile of 128 positions, 0 prunes it; the tiles of one index of ctx keep at most 2 tiles, and some such shard keeps exactly that many.
All inputs are finite; a program needn't handle non-finite values.
Results may differ from a plain program's by a relative error of at most 0.0065.
Values may be sent and summed in bfloat16 or wider, within the bound.
A program may use at most 576 MiB of HBM per device.

v0:
```python
import functools

import jax
import jax.numpy as jnp
from jax import lax
from jax.experimental import pallas as pl
from jax.experimental.pallas import tpu as pltpu
from jax.sharding import PartitionSpec as P

HEADS = 16
KV_HEADS = 8
HEAD_DIM = 128
WINDOW = 4096
BLK = 128
TILES_DEV = 4
SLOTS = 2
ROW = 8
BLOCKS = 64
GROUP = 2 * HEAD_DIM
MOST = 18
SIZES = (2, 4, 6, 8, 10, 12, 18)
PAD = MOST - 1
NQ = 3
NEG = -1e30
SCALE = 1.4426950408889634 / 12.0
MESH = pl.DeviceIdType.MESH
STEPS = ((0, 0), (0, 1), (1, 0), (3, 0), (1, 1), (3, 1), (2, 0), (2, 1))
Q_AFTER = 3


def place():
    c = lax.axis_index("ctx")
    return c, c // ROW, c % ROW


def peer(row, r):
    return {"ctx": row * ROW + r}


def ahead(r, step):
    dx, flip = STEPS[step]
    return (r // 2 + dx) % 4 * 2 + (r + flip) % 2


def behind(r, step):
    dx, flip = STEPS[step]
    return (r // 2 + 4 - dx) % 4 * 2 + (r + flip) % 2


def spread_kernel(
    kept_ref, q_hbm, k_hbm, v_hbm, qg, kvg,
    q_v, k_v, v_v, qs, kvs, in_sem, kv_send, kv_recv, q_send, q_recv, up_send, up_recv, own_sem,
):
    c, row, r = place()
    loads = [
        pltpu.make_async_copy(k_hbm, k_v, in_sem.at[0]),
        pltpu.make_async_copy(v_hbm, v_v, in_sem.at[1]),
        pltpu.make_async_copy(q_hbm, q_v, in_sem.at[2]),
    ]
    for load in loads:
        load.start()
    barrier = pltpu.get_barrier_semaphore()
    for step in range(1, ROW):
        pl.semaphore_signal(barrier, 1, device_id=peer(row, (r + step) % ROW), device_id_type=MESH)
    pl.semaphore_signal(barrier, 1, device_id=peer(1 - row, r), device_id_type=MESH)

    f = [kept_ref[c * TILES_DEV + j] > 0 for j in range(TILES_DEV)]

    def pick(ref, slot, cols):
        t = [ref[j * BLK : (j + 1) * BLK, cols] for j in range(TILES_DEV)]
        if slot == 0:
            return jnp.where(f[0], t[0], jnp.where(f[1], t[1], jnp.where(f[2], t[2], t[3])))
        return jnp.where(f[3], t[3], jnp.where(f[2], t[2], jnp.where(f[1], t[1], t[0])))

    def kv_copy(step):
        to = (r + step) % ROW
        return pltpu.make_async_remote_copy(
            kvs.at[to], kvg.at[ROW + r], kv_send.at[step], kv_recv.at[step],
            device_id=peer(row, to), device_id_type=MESH,
        )

    def q_copy(step):
        to = (r + step) % ROW
        return pltpu.make_async_remote_copy(
            qs.at[to], qg.at[r], q_send.at[step], q_recv.at[step],
            device_id=peer(row, to), device_id_type=MESH,
        )

    def up_copy(step):
        s = (r - step + ROW) % ROW
        src = kvs.at[r] if step == 0 else kvg.at[ROW + s]
        return pltpu.make_async_remote_copy(
            src, kvg.at[s], up_send.at[step], up_recv.at[step],
            device_id=peer(1 - row, r), device_id_type=MESH,
        )

    def pack_kv(h):
        cols = pl.ds(pl.multiple_of(h * HEAD_DIM, HEAD_DIM), HEAD_DIM)
        for slot in range(SLOTS):
            kvs[h, slot * BLK : (slot + 1) * BLK, :] = pick(k_v, slot, cols)
            kvs[h, (SLOTS + slot) * BLK : (SLOTS + slot + 1) * BLK, :] = pick(v_v, slot, cols).T

    def pack_q(h):
        for slot in range(SLOTS):
            for g in range(2):
                cols = pl.ds(pl.multiple_of(h * GROUP + g * HEAD_DIM, HEAD_DIM), HEAD_DIM)
                at = slot * 2 * BLK + g * BLK
                qs[h, :, at : at + BLK] = pick(q_v, slot, cols).T

    def kv_copy(step):
        to = ahead(r, step)
        return pltpu.make_async_remote_copy(
            kvs.at[to], kvg.at[ROW + r], kv_send.at[step], kv_recv.at[step],
            device_id=peer(row, to), device_id_type=MESH,
        )

    def q_copy(step):
        to = ahead(r, step)
        return pltpu.make_async_remote_copy(
            qs.at[to], qg.at[r], q_send.at[step], q_recv.at[step],
            device_id=peer(row, to), device_id_type=MESH,
        )

    def up_copy(step):
        s = behind(r, step)
        src = kvs.at[r] if step == 0 else kvg.at[ROW + s]
        return pltpu.make_async_remote_copy(
            src, kvg.at[s], up_send.at[step], up_recv.at[step],
            device_id=peer(1 - row, r), device_id_type=MESH,
        )

    def pass_up(step):
        @pl.when(row == 0)
        def _():
            up_copy(step).start()

    loads[0].wait()
    loads[1].wait()
    pack_kv(r)
    own_kv = pltpu.make_async_copy(kvs.at[r], kvg.at[ROW + r], own_sem.at[0])
    own_kv.start()
    pack_kv(ahead(r, 1))
    pl.semaphore_wait(barrier, ROW)
    pass_up(0)
    for step in range(1, ROW):
        if step > 1:
            pack_kv(ahead(r, step))
        kv_copy(step).start()
    loads[2].wait()
    for step in range(ROW):
        pack_q(ahead(r, step))
    own_q = pltpu.make_async_copy(qs.at[r], qg.at[r], own_sem.at[1])
    own_q.start()
    for step in range(1, ROW):
        kv_copy(step).wait_recv()
        pass_up(step)
        if step == Q_AFTER:
            for other in range(1, ROW):
                q_copy(other).start()
    for step in range(1, ROW):
        q_copy(step).wait_recv()

    @pl.when(row == 1)
    def _():
        for step in range(ROW):
            up_copy(step).wait_recv()

    @pl.when(row == 0)
    def _():
        for step in range(ROW):
            up_copy(step).wait_send()

    for step in range(1, ROW):
        kv_copy(step).wait_send()
        q_copy(step).wait_send()
    own_kv.wait()
    own_q.wait()


def spread(kept, q, k, v):
    rows = q.shape[0]
    anywhere = pl.BlockSpec(memory_space=pl.ANY)
    bf16 = jnp.bfloat16
    dma = pltpu.SemaphoreType.DMA
    return pl.pallas_call(
        spread_kernel,
        out_shape=(
            jax.ShapeDtypeStruct((ROW, HEAD_DIM, SLOTS * 2 * BLK), bf16),
            jax.ShapeDtypeStruct((2 * ROW, 2 * SLOTS * BLK, HEAD_DIM), bf16),
        ),
        in_specs=[pl.BlockSpec(memory_space=pltpu.SMEM), anywhere, anywhere, anywhere],
        out_specs=(anywhere, anywhere),
        scratch_shapes=[
            pltpu.VMEM((rows, HEADS * HEAD_DIM), bf16),
            pltpu.VMEM((rows, KV_HEADS * HEAD_DIM), bf16),
            pltpu.VMEM((rows, KV_HEADS * HEAD_DIM), bf16),
            pltpu.VMEM((ROW, HEAD_DIM, SLOTS * 2 * BLK), bf16),
            pltpu.VMEM((ROW, 2 * SLOTS * BLK, HEAD_DIM), bf16),
            dma((3,)), dma((ROW,)), dma((ROW,)), dma((ROW,)), dma((ROW,)), dma((ROW,)), dma((ROW,)), dma((2,)),
        ],
        compiler_params=pltpu.CompilerParams(
            collective_id=1, has_side_effects=True, vmem_limit_bytes=60 << 20
        ),
        name="spread",
    )(kept, q, k, v)


def attend_kernel(
    parents_ref, kept_ref, qg, kvg, og,
    q_v, kv_v, o_v, bias_ref, up_ref, base_ref, list_ref, seen_ref, size_ref, in_sem, out_sem,
):
    c, row, r = place()
    half = ROW * 2 * SLOTS * BLK
    load_own = pltpu.make_async_copy(kvg.at[half:], kv_v.at[half:], in_sem.at[0])
    load_low = pltpu.make_async_copy(kvg.at[:half], kv_v.at[:half], in_sem.at[1])
    load_q = pltpu.make_async_copy(qg, q_v, in_sem.at[2])
    load_q.start()
    load_own.start()

    @pl.when(row == 1)
    def _():
        load_low.start()

    end = BLOCKS
    reach = WINDOW // BLK
    first_tile = row * ROW * TILES_DEV

    up_ref[end] = -BLOCKS * 4
    up_ref[0] = end
    for t in range(1, BLOCKS):
        p = parents_ref[t]
        up_ref[t] = jnp.where(kept_ref[p] > 0, p, up_ref[p])
    base_ref[end] = half
    for s in range(BLOCKS // TILES_DEV):
        lin = jnp.clip(s - ROW * row + ROW, 0, 2 * ROW - 1) * (2 * SLOTS * BLK)
        before = jnp.int32(0)
        for j in range(TILES_DEV):
            t = s * TILES_DEV + j
            base_ref[t] = lin + jnp.minimum(before, SLOTS - 1) * BLK
            before = before + jnp.where(kept_ref[t] > 0, 1, 0)
    count = jnp.int32(0)
    for j in range(ROW * TILES_DEV):
        t = first_tile + j
        list_ref[count] = t
        count = count + jnp.where(kept_ref[t] > 0, 1, 0)

    def gather(i, _):
        t = list_ref[i]

        def visit(state):
            node, k = state
            seen_ref[i * MOST + k] = base_ref[node] + jnp.where(t - node == reach, 2, 0)
            nxt = up_ref[node]
            return jnp.where(nxt >= t - reach, nxt, end), k + 1

        _, k = lax.while_loop(lambda state: state[0] < end, visit, (t, jnp.int32(0)))
        size_ref[i] = k
        for extra in range(PAD):
            seen_ref[i * MOST + k + extra] = base_ref[end] + 1
        return 0

    lax.fori_loop(0, count, gather, 0)
    rc = lax.broadcasted_iota(jnp.int32, (BLK, BLK), 1) - lax.broadcasted_iota(jnp.int32, (BLK, BLK), 0)
    bias_ref[0] = jnp.zeros((BLK, BLK), jnp.float32)
    bias_ref[1] = jnp.full((BLK, BLK), NEG, jnp.float32)
    bias_ref[2] = jnp.where(rc < 0, 0.0, NEG)
    bias_ref[3] = jnp.where(rc >= 0, 0.0, NEG)
    load_q.wait()
    load_own.wait()

    @pl.when(row == 1)
    def _():
        load_low.wait()

    def some(j, _):
        which = [jnp.minimum(NQ * j + n, count - 1) for n in range(NQ)]
        spots, heads = [], []
        for i in which:
            t = list_ref[i]
            slot = (base_ref[t] // BLK) % SLOTS
            shard = (t - first_tile) // TILES_DEV
            spots.append((shard, pl.multiple_of(slot * BLK, BLK)))
            heads.append(q_v[shard, :, pl.ds(pl.multiple_of(slot * 2 * BLK, 2 * BLK), 2 * BLK)])
        longest = functools.reduce(jnp.maximum, [size_ref[i] for i in which])

        def over(size):
            parts = [[] for _ in which]
            tops = [None for _ in which]
            values = [[] for _ in which]
            for n, i in enumerate(which):
                for g in range(size):
                    entry = seen_ref[i * MOST + g]
                    base = pl.multiple_of(entry // BLK * BLK, BLK)
                    bias = bias_ref[3 if g == 0 else entry % BLK]
                    s = jnp.dot(kv_v[pl.ds(base, BLK), :], heads[n], preferred_element_type=jnp.float32) * SCALE
                    s = s + jnp.concatenate([bias, bias], 1)
                    fold = jnp.max(s.reshape(BLK // 8, 8, 2 * BLK), axis=0)
                    tops[n] = fold if g == 0 else jnp.maximum(tops[n], fold)
                    parts[n].append(s)
                    values[n].append(kv_v[pl.ds(base + SLOTS * BLK, BLK), :])
            tops = [jnp.max(top, axis=0, keepdims=True) for top in tops]
            accs, totals = [], []
            for n in range(NQ):
                weights, total = [], None
                for part in parts[n]:
                    term = jnp.exp2(part - tops[n])
                    fold = jnp.sum(term.reshape(BLK // 8, 8, 2 * BLK), axis=0)
                    total = fold if total is None else total + fold
                    weights.append(term.astype(jnp.bfloat16))
                totals.append(jnp.sum(total, axis=0, keepdims=True))
                w = jnp.concatenate(weights, 0)
                accs.append(jnp.dot(jnp.concatenate(values[n], 1), w, preferred_element_type=jnp.float32))
            outs = [(acc / total).astype(jnp.bfloat16) for acc, total in zip(accs, totals)]
            outs = [jnp.concatenate([o[:, :BLK].T, o[:, BLK:].T], 1) for o in outs]
            for i, o in zip(which, outs):
                o_v[i] = o

        for low, size in zip((0, *SIZES), SIZES):
            pl.when((longest > low) & (longest <= size))(functools.partial(over, size))
        for n in range(NQ):

            @pl.when(NQ * j + n < count)
            def _():
                shard, at = spots[n]
                pltpu.make_async_copy(
                    o_v.at[which[n]], og.at[shard, pl.ds(at, BLK), :], out_sem.at[which[n]]
                ).start()

        return 0

    lax.fori_loop(0, (count + NQ - 1) // NQ, some, 0)

    def drain(w, _):
        pltpu.make_async_copy(o_v.at[w], og.at[0, pl.ds(0, BLK), :], out_sem.at[w]).wait()
        return 0

    lax.fori_loop(0, count, drain, 0)


def attend(parents, kept, qg, kvg):
    smem = pl.BlockSpec(memory_space=pltpu.SMEM)
    anywhere = pl.BlockSpec(memory_space=pl.ANY)
    bf16 = jnp.bfloat16
    rows = 2 * ROW * 2 * SLOTS * BLK
    return pl.pallas_call(
        attend_kernel,
        out_shape=jax.ShapeDtypeStruct((ROW, SLOTS * BLK, GROUP), bf16),
        in_specs=[smem, smem, anywhere, anywhere],
        out_specs=anywhere,
        scratch_shapes=[
            pltpu.VMEM((ROW, HEAD_DIM, SLOTS * 2 * BLK), bf16),
            pltpu.VMEM((rows, HEAD_DIM), bf16),
            pltpu.VMEM((ROW * SLOTS, BLK, GROUP), bf16),
            pltpu.VMEM((4, BLK, BLK), jnp.float32),
            pltpu.SMEM((BLOCKS + 1,), jnp.int32),
            pltpu.SMEM((BLOCKS + 1,), jnp.int32),
            pltpu.SMEM((ROW * TILES_DEV + 1,), jnp.int32),
            pltpu.SMEM((ROW * SLOTS * MOST + PAD,), jnp.int32),
            pltpu.SMEM((ROW * SLOTS,), jnp.int32),
            pltpu.SemaphoreType.DMA((3,)),
            pltpu.SemaphoreType.DMA((ROW * SLOTS,)),
        ],
        compiler_params=pltpu.CompilerParams(vmem_limit_bytes=60 << 20),
        name="attend",
    )(parents, kept, qg, kvg.reshape(rows, HEAD_DIM))


def collect_kernel(og, oc, send, recv, own_sem):
    _, row, r = place()
    barrier = pltpu.get_barrier_semaphore()
    for step in range(1, ROW):
        pl.semaphore_signal(barrier, 1, device_id=peer(row, (r + step) % ROW), device_id_type=MESH)
    own = pltpu.make_async_copy(og.at[r], oc.at[r], own_sem)
    own.start()
    pl.semaphore_wait(barrier, ROW - 1)
    copies = []
    for step in range(1, ROW):
        to = (r + step) % ROW
        copies.append(
            pltpu.make_async_remote_copy(
                og.at[to], oc.at[r], send.at[step], recv.at[step],
                device_id=peer(row, to), device_id_type=MESH,
            )
        )
    for copy in copies:
        copy.start()
    for copy in copies:
        copy.wait_recv()
    for copy in copies:
        copy.wait_send()
    own.wait()


def collect(og):
    anywhere = pl.BlockSpec(memory_space=pl.ANY)
    return pl.pallas_call(
        collect_kernel,
        out_shape=jax.ShapeDtypeStruct((ROW, SLOTS * BLK, GROUP), jnp.bfloat16),
        in_specs=[anywhere],
        out_specs=anywhere,
        scratch_shapes=[
            pltpu.SemaphoreType.DMA((ROW,)), pltpu.SemaphoreType.DMA((ROW,)), pltpu.SemaphoreType.DMA,
        ],
        compiler_params=pltpu.CompilerParams(
            collective_id=2, has_side_effects=True, vmem_limit_bytes=60 << 20
        ),
        name="collect",
    )(og)


def expand_kernel(kept_ref, oc, out, wide, sem):
    c, _, _ = place()
    copies = []
    before = jnp.bool_(False)
    for j in range(TILES_DEV):
        rows = slice(j * BLK, (j + 1) * BLK)
        kept = kept_ref[c * TILES_DEV + j] > 0
        slot = pl.multiple_of(jnp.where(before, BLK, 0), BLK)

        @pl.when(kept)
        def _():
            for h in range(ROW):
                wide[rows, h * GROUP : (h + 1) * GROUP] = oc[h, pl.ds(slot, BLK), :]

        @pl.when(jnp.logical_not(kept))
        def _():
            wide[rows, :] = jnp.zeros((BLK, HEADS * HEAD_DIM), jnp.bfloat16)

        before = before | kept
        copies.append(pltpu.make_async_copy(wide.at[rows], out.at[rows], sem.at[j]))
        copies[-1].start()
    for copy in copies:
        copy.wait()


def expand(kept, oc):
    rows = TILES_DEV * BLK
    return pl.pallas_call(
        expand_kernel,
        out_shape=jax.ShapeDtypeStruct((rows, HEADS * HEAD_DIM), jnp.bfloat16),
        in_specs=[pl.BlockSpec(memory_space=pltpu.SMEM), pl.BlockSpec(memory_space=pltpu.VMEM)],
        out_specs=pl.BlockSpec(memory_space=pl.ANY),
        scratch_shapes=[
            pltpu.VMEM((rows, HEADS * HEAD_DIM), jnp.bfloat16), pltpu.SemaphoreType.DMA((TILES_DEV,)),
        ],
        name="expand",
    )(kept, oc)


def body(queries, key_rows, value_rows, parents, kept_tiles):
    qg, kvg = spread(kept_tiles, queries, key_rows, value_rows)
    og = attend(parents, kept_tiles, qg, kvg)
    return expand(kept_tiles, collect(og))


def solution(mesh):
    return jax.shard_map(
        body,
        mesh=mesh,
        in_specs=(
            P(("dp", "ctx"), None),
            P(("dp", "ctx"), None),
            P(("dp", "ctx"), None),
            P("dp"),
            P("dp"),
        ),
        out_specs=P(("dp", "ctx"), None),
        check_vma=False,
    )
```

profile of v0, /device:TPU:1, one launch (start us, length us, event | category | flops | bytes accessed | tf_op | source)
XLA Modules:
  0.0 60.0 jit_solution(1374824633692987772)
XLA Ops:
  0.0 31.5 %spread.1 = (bf16[8,128,512]{2,1,0:T(8,128)(2,1)}, bf16[16,512,128]{2,1,0:T(8,128)(2,1)}) custom-call(s32[64]{0:T(128)} %kept_ref.5, bf16[512,2048]{1,0:T(8,128)(2,1)} %q_hbm.1, bf16[512,1024]{1,0:T(8,128)(2,1)} %k_hbm.1, bf16[512,1024]{1,0:T(8,128)(2,1)} %v_hbm.1), custom_call_target="tpu_custom_call" | custom-call | tf_op jit(solution)/shard_map/spread/pallas_call | solution.py:185
  31.5 9.9 %attend.1.og = bf16[8,256,256]{2,1,0:T(8,128)(2,1)} custom-call(s32[64]{0:T(128)} %parents_ref.1, s32[64]{0:T(128)} %kept_ref.5, bf16[8,128,512]{2,1,0:T(8,128)(2,1)} %get-tuple-element.7.qg, bf16[8192,128]{1,0:T(8,128)(2,1)} %bitcast.1), custom_call_target="tpu_custom_call" | custom-call | tf_op jit(solution)/shard_map/attend/pallas_call | solution.py:345
  41.4 15.8 %collect.1.oc = bf16[8,256,256]{2,1,0:T(8,128)(2,1)} custom-call(bf16[8,256,256]{2,1,0:T(8,128)(2,1)} %attend.1.og), custom_call_target="tpu_custom_call" | custom-call | tf_op jit(solution)/shard_map/collect/pallas_call | solution.py:396
  57.2 2.6 %expand.1 = bf16[512,2048]{1,0:T(8,128)(2,1)} custom-call(s32[64]{0:T(128)} %kept_ref.5, bf16[8,256,256]{2,1,0:T(8,128)(2,1)} %collect.1.oc), custom_call_target="tpu_custom_call" | custom-call | tf_op jit(solution)/shard_map/expand/pallas_call | solution.py:438
where the time goes:
time: 60.2 us; the launch traced here: 60 us
  Pallas kernels  59.8 us (99%)
    pallas_call x1, Pallas kernels, spread(): pl.pallas_call(spread_kernel, out_shape=(jax.ShapeDtypeStruct((ROW, HEAD_...  31.5 us
    pallas_call x1, Pallas kernels, collect(): pl.pallas_call(collect_kernel, out_shape=jax.ShapeDtypeStruct((ROW, SLOTS...  15.8 us
    pallas_call x1, Pallas kernels, attend(): pl.pallas_call(attend_kernel, out_shape=jax.ShapeDtypeStruct((ROW, SLOTS...  9.93 us
    pallas_call x1, Pallas kernels, expand(): pl.pallas_call(expand_kernel, out_shape=jax.ShapeDtypeStruct((rows, HEADS...  2.63 us

commit v1 on v0

--- a/solution.py
+++ b/solution.py
@@ -20,7 +20,8 @@
 MOST = 18
 SIZES = (2, 4, 6, 8, 10, 12, 18)
 PAD = MOST - 1
-NQ = 3
+WIDE = 4
+NARROW = 2
 NEG = -1e30
 SCALE = 1.4426950408889634 / 12.0
 MESH = pl.DeviceIdType.MESH
@@ -272,8 +273,8 @@
     def _():
         load_low.wait()
 
-    def some(j, _):
-        which = [jnp.minimum(NQ * j + n, count - 1) for n in range(NQ)]
+    def some(width, first, j, _):
+        which = [jnp.minimum(first + width * j + n, count - 1) for n in range(width)]
         spots, heads = [], []
         for i in which:
             t = list_ref[i]
@@ -300,7 +301,7 @@
                     values[n].append(kv_v[pl.ds(base + SLOTS * BLK, BLK), :])
             tops = [jnp.max(top, axis=0, keepdims=True) for top in tops]
             accs, totals = [], []
-            for n in range(NQ):
+            for n in range(width):
                 weights, total = [], None
                 for part in parts[n]:
                     term = jnp.exp2(part - tops[n])
@@ -317,9 +318,9 @@
 
         for low, size in zip((0, *SIZES), SIZES):
             pl.when((longest > low) & (longest <= size))(functools.partial(over, size))
-        for n in range(NQ):
-
-            @pl.when(NQ * j + n < count)
+        for n in range(width):
+
+            @pl.when(first + width * j + n < count)
             def _():
                 shard, at = spots[n]
                 pltpu.make_async_copy(
@@ -328,7 +329,10 @@
 
         return 0
 
-    lax.fori_loop(0, (count + NQ - 1) // NQ, some, 0)
+    many = count // WIDE
+    lax.fori_loop(0, many, functools.partial(some, WIDE, 0), 0)
+    left = count - WIDE * many
+    lax.fori_loop(0, (left + NARROW - 1) // NARROW, functools.partial(some, NARROW, WIDE * many), 0)
 
     def drain(w, _):
         pltpu.make_async_copy(o_v.at[w], og.at[0, pl.ds(0, BLK), :], out_sem.at[w]).wait()

time: 60.2 us -> 58.5 us (0.972)
  the two profiles are of different devices: /device:TPU:1 before, /device:TPU:17 now
where the time goes in v1:
time: 58.5 us; the launch traced here: 58.3 us
  Pallas kernels  58.1 us (99%)
    pallas_call x1, Pallas kernels, spread(): pl.pallas_call(spread_kernel, out_shape=(jax.ShapeDtypeStruct((ROW, HEAD_...  29.4 us
    pallas_call x1, Pallas kernels, collect(): pl.pallas_call(collect_kernel, out_shape=jax.ShapeDtypeStruct((ROW, SLOTS...  15.9 us
    pallas_call x1, Pallas kernels, attend(): pl.pallas_call(attend_kernel, out_shape=jax.ShapeDtypeStruct((ROW, SLOTS...  10.2 us
    pallas_call x1, Pallas kernels, expand(): pl.pallas_call(expand_kernel, out_shape=jax.ShapeDtypeStruct((rows, HEADS...  2.63 us

profile of v1, /device:TPU:17, one launch (start us, length us, event | category | flops | bytes accessed | tf_op | source)
XLA Modules:
  0.0 58.3 jit_solution(9191470024469463387)
XLA Ops:
  0.0 29.4 %spread.1 = (bf16[8,128,512]{2,1,0:T(8,128)(2,1)}, bf16[16,512,128]{2,1,0:T(8,128)(2,1)}) custom-call(s32[64]{0:T(128)} %kept_ref.5, bf16[512,2048]{1,0:T(8,128)(2,1)} %q_hbm.1, bf16[512,1024]{1,0:T(8,128)(2,1)} %k_hbm.1, bf16[512,1024]{1,0:T(8,128)(2,1)} %v_hbm.1), custom_call_target="tpu_custom_call" | custom-call | tf_op jit(solution)/shard_map/spread/pallas_call | solution.py:186
  29.4 10.2 %attend.1.og = bf16[8,256,256]{2,1,0:T(8,128)(2,1)} custom-call(s32[64]{0:T(128)} %parents_ref.1, s32[64]{0:T(128)} %kept_ref.5, bf16[8,128,512]{2,1,0:T(8,128)(2,1)} %get-tuple-element.7.qg, bf16[8192,128]{1,0:T(8,128)(2,1)} %bitcast.1), custom_call_target="tpu_custom_call" | custom-call | tf_op jit(solution)/shard_map/attend/pallas_call | solution.py:349
  39.6 15.9 %collect.1.oc = bf16[8,256,256]{2,1,0:T(8,128)(2,1)} custom-call(bf16[8,256,256]{2,1,0:T(8,128)(2,1)} %attend.1.og), custom_call_target="tpu_custom_call" | custom-call | tf_op jit(solution)/shard_map/collect/pallas_call | solution.py:400
  55.5 2.6 %expand.1 = bf16[512,2048]{1,0:T(8,128)(2,1)} custom-call(s32[64]{0:T(128)} %kept_ref.5, bf16[8,256,256]{2,1,0:T(8,128)(2,1)} %collect.1.oc), custom_call_target="tpu_custom_call" | custom-call | tf_op jit(solution)/shard_map/expand/pallas_call | solution.py:442

commit v2 on v1

--- a/solution.py
+++ b/solution.py
@@ -329,9 +329,9 @@
 
         return 0
 
-    many = count // WIDE
+    many = (count + 1) // WIDE
     lax.fori_loop(0, many, functools.partial(some, WIDE, 0), 0)
-    left = count - WIDE * many
+    left = jnp.maximum(count - WIDE * many, 0)
     lax.fori_loop(0, (left + NARROW - 1) // NARROW, functools.partial(some, NARROW, WIDE * many), 0)
 
     def drain(w, _):

time: 58.5 us -> 57.4 us (0.981)
  the two profiles are of different devices: /device:TPU:17 before, /device:TPU:1 now
where the time goes in v2:
time: 57.4 us; the launch traced here: 56.9 us
  Pallas kernels  56.7 us (99%)
    pallas_call x1, Pallas kernels, spread(): pl.pallas_call(spread_kernel, out_shape=(jax.ShapeDtypeStruct((ROW, HEAD_...  31.5 us
    pallas_call x1, Pallas kernels, collect(): pl.pallas_call(collect_kernel, out_shape=jax.ShapeDtypeStruct((ROW, SLOTS...  15.8 us
    pallas_call x1, Pallas kernels, attend(): pl.pallas_call(attend_kernel, out_shape=jax.ShapeDtypeStruct((ROW, SLOTS...  6.75 us
    pallas_call x1, Pallas kernels, expand(): pl.pallas_call(expand_kernel, out_shape=jax.ShapeDtypeStruct((rows, HEADS...  2.64 us

profile of v2, /device:TPU:1, one launch (start us, length us, event | category | flops | bytes accessed | tf_op | source)
XLA Modules:
  0.0 56.9 jit_solution(606346033762137716)
XLA Ops:
  0.0 31.5 %spread.1 = (bf16[8,128,512]{2,1,0:T(8,128)(2,1)}, bf16[16,512,128]{2,1,0:T(8,128)(2,1)}) custom-call(s32[64]{0:T(128)} %kept_ref.5, bf16[512,2048]{1,0:T(8,128)(2,1)} %q_hbm.1, bf16[512,1024]{1,0:T(8,128)(2,1)} %k_hbm.1, bf16[512,1024]{1,0:T(8,128)(2,1)} %v_hbm.1), custom_call_target="tpu_custom_call" | custom-call | tf_op jit(solution)/shard_map/spread/pallas_call | solution.py:186
  31.5 6.8 %attend.1.og = bf16[8,256,256]{2,1,0:T(8,128)(2,1)} custom-call(s32[64]{0:T(128)} %parents_ref.1, s32[64]{0:T(128)} %kept_ref.5, bf16[8,128,512]{2,1,0:T(8,128)(2,1)} %get-tuple-element.7.qg, bf16[8192,128]{1,0:T(8,128)(2,1)} %bitcast.1), custom_call_target="tpu_custom_call" | custom-call | tf_op jit(solution)/shard_map/attend/pallas_call | solution.py:349
  38.2 15.8 %collect.1.oc = bf16[8,256,256]{2,1,0:T(8,128)(2,1)} custom-call(bf16[8,256,256]{2,1,0:T(8,128)(2,1)} %attend.1.og), custom_call_target="tpu_custom_call" | custom-call | tf_op jit(solution)/shard_map/collect/pallas_call | solution.py:400
  54.0 2.6 %expand.1 = bf16[512,2048]{1,0:T(8,128)(2,1)} custom-call(s32[64]{0:T(128)} %kept_ref.5, bf16[8,256,256]{2,1,0:T(8,128)(2,1)} %collect.1.oc), custom_call_target="tpu_custom_call" | custom-call | tf_op jit(solution)/shard_map/expand/pallas_call | solution.py:442
